TPU v7x, 512 devices: a whole 4x8x8 slice. The times are simulated.
512 devices in a mesh: sec: 64 (over x, y, core), mp: 8 (over z).
Axes of the slice: x: 4, y: 8, z: 8, core: 2. Of those that a mesh axis runs over, the one named last changes fastest.
Arguments:
- inputs: bfloat16 [8192, 2048], P('sec'), may hold values from -6 to 6
- expert_w: bfloat16 [8, 2048, 1024], P('mp', 'sec'), may hold values from -0.125 to 0.125
- gate_w: bfloat16 [2048, 6, 8], replicated, may hold values from -0.125 to 0.125
- tower_up: bfloat16 [64, 1024, 4096], P('sec', None, 'mp'), as said below
- tower_out: bfloat16 [64, 4096], P('sec', 'mp'), as said below
- sections: int32 [64], replicated, may hold values from 0 to 5, as said below
- tasks: int32 [8192, 6], P('sec'), may hold values from 0 to 1, as said below
- labels: int32 [8192, 6], P('sec'), may hold values 0 or 1
Outputs:
- input_grad: bfloat16 [8192, 2048], P('sec', 'mp')
Inputs may be any that keep to these rules, and one draw needn't show every extreme that they name: `sections`: each task owns one run of consecutive indices, the runs in task order, every task at least one index. `tasks`: in each aligned block of 128 examples, task t has at most 4 times as many examples as its section has indices of sec; every task reaches this bound in some block. `tower_up`: all indices of one section hold equal copies. `tower_out`: all indices of one section hold equal copies.
All inputs are finite; a program needn't handle non-finite values. No bound on the sum of `labels` on one device may be relied on, other than what follows from the above.
Results may differ from a plain program's by a relative error of at most 0.024.
Values may be sent and summed in bfloat16 or wider, within the bound.
No kernel may reach another device: no remote copies, remote signals or barrier semaphores. Data moves between devices by JAX's collectives and lax.ppermute only.
A program may use at most 64 MiB of HBM per device.

v0:
```python
import jax
import jax.numpy as jnp
from jax import lax
from jax.sharding import PartitionSpec as P

loss_scale = 64.0


def silu_slope(value, sig):
    return sig * (1.0 + value * (1.0 - sig))


def per_device(inputs, expert_w, gate_w, tower_up, tower_out, sections, tasks, labels):
    rows = inputs.shape[0]
    task_count = tasks.shape[1]
    n_sec = lax.axis_size("sec")
    pair_slots = 2 * rows // n_sec
    slots = n_sec * pair_slots
    local_w = expert_w[0]
    width = local_w.shape[1]
    picker = (jnp.arange(gate_w.shape[2], dtype=jnp.int32) == lax.axis_index("mp")).astype(
        jnp.float32
    )
    gate_logit = jnp.einsum("nd,dtk->ntk", inputs, gate_w, preferred_element_type=jnp.float32)
    raised = jnp.exp(gate_logit)
    gates = raised / jnp.sum(raised, axis=2, keepdims=True)
    mine = jnp.sum(gates * picker, axis=2)
    whole_w = lax.all_gather(local_w, "sec", axis=0, tiled=True)
    pre = jnp.dot(inputs, whole_w, preferred_element_type=jnp.float32)
    sig_pre = jax.nn.sigmoid(pre)
    expert_out = (pre * sig_pre).astype(jnp.bfloat16)
    task_ids = jnp.arange(task_count, dtype=jnp.int32)
    members = jnp.sum((sections[None, :] == task_ids[:, None]).astype(jnp.int32), axis=1)
    first = jnp.sum((sections[None, :] < task_ids[:, None]).astype(jnp.int32), axis=1)
    ranks = jnp.cumsum(tasks, axis=0) - tasks
    target = first[None, :] + ranks % members[None, :]
    place = target * pair_slots + ranks // members[None, :]
    place = jnp.where(tasks > 0, place, slots)
    pair_total = rows * task_count
    pair_ids = jnp.arange(pair_total, dtype=jnp.int32)
    source = (
        jnp.full((slots,), pair_total, jnp.int32).at[place.reshape(-1)].set(pair_ids, mode="drop")
    )
    filled = (source < pair_total).astype(jnp.float32)
    source = jnp.minimum(source, pair_total - 1)
    src_row = source // task_count
    src_task = source % task_count
    weight = mine[src_row, src_task] * filled
    contrib = weight[:, None] * expert_out[src_row].astype(jnp.float32)
    tag_out = (filled * (1.0 + labels[src_row, src_task].astype(jnp.float32))).astype(jnp.bfloat16)
    sent = lax.psum(contrib.astype(jnp.bfloat16), "mp")
    arrived, tag_in = (
        lax.all_to_all(
            sent.reshape(n_sec, pair_slots, -1), "sec", split_axis=0, concat_axis=0, tiled=True
        ),
        lax.all_to_all(
            tag_out.reshape(n_sec, pair_slots), "sec", split_axis=0, concat_axis=0, tiled=True
        ),
    )
    arrived = arrived.reshape(slots, -1)
    up_local = tower_up[0]
    out_local = tower_out[0].astype(jnp.float32)
    act = jnp.dot(arrived, up_local, preferred_element_type=jnp.float32)
    sig_act = jax.nn.sigmoid(act)
    partial_logit = jnp.sum(act * sig_act * out_local[None, :], axis=1)
    logit = lax.psum(partial_logit, "mp")
    tag_value = tag_in.reshape(slots).astype(jnp.float32)
    alive = (tag_value > 0.5).astype(jnp.float32)
    label_value = jnp.maximum(tag_value - 1.0, 0.0)
    slope = loss_scale * (jax.nn.sigmoid(logit) - label_value) * alive
    act_grad = (slope[:, None] * out_local[None, :] * silu_slope(act, sig_act)).astype(jnp.bfloat16)
    back = lax.dot_general(
        act_grad, up_local, (((1,), (1,)), ((), ())), preferred_element_type=jnp.float32
    )
    grads = lax.psum(back.astype(jnp.bfloat16), "mp")
    returned = lax.all_to_all(
        grads.reshape(n_sec, pair_slots, -1), "sec", split_axis=0, concat_axis=0, tiled=True
    ).reshape(slots, -1)
    padded = jnp.concatenate([returned, jnp.zeros((1, width), jnp.bfloat16)], axis=0)
    mixture_grad = padded[place]
    expert_grad = jnp.zeros((rows, width), jnp.float32)
    for task in range(task_count):
        expert_grad = expert_grad + mine[:, task : task + 1] * mixture_grad[:, task].astype(
            jnp.float32
        )
    gate_grad = jnp.einsum(
        "nte,ne->nt", mixture_grad, expert_out, preferred_element_type=jnp.float32
    )
    spread_sum = lax.psum(mine * gate_grad, "mp")
    gate_logit_grad = mine * (gate_grad - spread_sum)
    pre_grad = (expert_grad * silu_slope(pre, sig_pre)).astype(jnp.bfloat16)
    gate_cols = jnp.sum(gate_w.astype(jnp.float32) * picker, axis=2)
    gate_part = jnp.dot(gate_logit_grad, gate_cols.T, precision=lax.Precision.HIGHEST)
    input_part = lax.dot_general(
        pre_grad, whole_w, (((1,), (1,)), ((), ())), preferred_element_type=jnp.float32
    )
    return lax.psum_scatter(
        (input_part + gate_part).astype(jnp.bfloat16), "mp", scatter_dimension=1, tiled=True
    )


def solution(mesh):
    in_specs = (
        P("sec", None),
        P("mp", "sec", None),
        P(),
        P("sec", None, "mp"),
        P("sec", "mp"),
        P(),
        P("sec", None),
        P("sec", None),
    )
    out_specs = P("sec", "mp")
    return jax.shard_map(
        per_device, mesh=mesh, in_specs=in_specs, out_specs=out_specs, check_vma=False
    )
```

profile of v0, /device:TPU:2, one launch (start us, length us, event | category | flops | bytes accessed | tf_op | source)
XLA Modules:
  0.0 409.1 jit_solution(17913889090033370645)
XLA Ops:
  9.9 1.3 compare_select_fusion
  11.4 3.4 scatter_custom_fusion
  14.8 1.4 fusion.54
  16.3 1.4 gather_fusion.1
  17.6 1.4 gather_fusion
  19.1 79.5 %all-gather.3.cloned.1.call-done = bf16[1,2048,1024]{2,1,0:T(8,128)(2,1)} async-done(((bf16[1,32,1024]{2,1,0:T(8,128)(2,1)}), bf16[1,2048,1024]{2,1,0:T(8,128)(2,1)}) %all-gather.3.cloned.1.call-update) | async-done | bytes 4194320 | tf_op jit(solution)/shard_map/all_gather | solution.py:28
  98.6 3.8 multiply_convert_fusion.2
  102.4 1.2 gather_fusion.2
  104.9 16.0 %all_to_all.20 = bf16[64,1,4]{2,1,0:T(2,128)(2,1)S(1)} all-to-all(bf16[64,1,4]{2,1,0:T(2,128)(2,1)S(1)} %all_to_all.16), channel_id=1, replica_groups=mesh['sec'=64,'mp'=8] {'sec'}, dimensions={0} | all-to-all | bytes 1024 | tf_op jit(solution)/shard_map/all_to_all | solution.py:56
  120.8 62.6 %all-reduce.4.cloned.1.call-done = bf16[64,4,1024]{2,1,0:T(4,128)(2,1)} async-done(((bf16[64,4,1024]{2,1,0:T(4,128)(2,1)}), bf16[64,4,1024]{2,1,0:T(4,128)(2,1)}) %all-reduce.4.cloned.1.call-update) | async-done | bytes 524304 | tf_op jit(solution)/shard_map/psum | solution.py:51
  183.4 10.3 %all-to-all-start.1 = ((bf16[64,4,1024]{2,1,0:T(4,128)(2,1)}), bf16[64,4,1024]{2,1,0:T(4,128)(2,1)S(1)}, u32[]{:S(2)}, u32[]{:S(2)}) async-start(bf16[64,4,1024]{2,1,0:T(4,128)(2,1)} %all-reduce.4.cloned.1.call-done), calls=%async_computation.1 | async-start | bytes 1048576 | tf_op jit(solution)/shard_map/all_to_all | solution.py:53
  194.3 16.1 %all-to-all-done.1 = bf16[64,4,1024]{2,1,0:T(4,128)(2,1)S(1)} async-done(((bf16[64,4,1024]{2,1,0:T(4,128)(2,1)}), bf16[64,4,1024]{2,1,0:T(4,128)(2,1)S(1)}, u32[]{:S(2)}, u32[]{:S(2)}) %all-to-all-start.1) | async-done | bytes 524320 | tf_op jit(solution)/shard_map/all_to_all | solution.py:53
  211.1 16.3 %psum.29 = f32[256]{0:T(256)S(1)} all-reduce(f32[256]{0:T(256)S(1)} %get-tuple-element.29), channel_id=1, replica_groups=mesh['sec'=64,'mp'=8] {'mp'}, use_global_device_ids=true, to_apply=%region_8.9 | all-reduce | flops 256 | bytes 2048 | tf_op jit(solution)/shard_map/psum | solution.py:66
  229.1 75.2 %all-reduce.6.cloned.1.call-done = bf16[64,4,1024]{2,1,0:T(4,128)(2,1)} async-done(((bf16[64,4,1024]{2,1,0:T(4,128)(2,1)}), bf16[64,4,1024]{2,1,0:T(4,128)(2,1)}) %all-reduce.6.cloned.1.call-update) | async-done | bytes 524304 | tf_op jit(solution)/shard_map/psum | solution.py:75
  304.4 10.3 %all-to-all-start.2 = ((bf16[64,4,1024]{2,1,0:T(4,128)(2,1)}), bf16[64,4,1024]{2,1,0:T(4,128)(2,1)S(1)}, u32[]{:S(2)}, u32[]{:S(2)}) async-start(bf16[64,4,1024]{2,1,0:T(4,128)(2,1)} %all-reduce.6.cloned.1.call-done), calls=%async_computation.2 | async-start | bytes 1048576 | tf_op jit(solution)/shard_map/all_to_all | solution.py:76
  315.8 15.5 %all-to-all-done.2 = bf16[64,4,1024]{2,1,0:T(4,128)(2,1)S(1)} async-done(((bf16[64,4,1024]{2,1,0:T(4,128)(2,1)}), bf16[64,4,1024]{2,1,0:T(4,128)(2,1)S(1)}, u32[]{:S(2)}, u32[]{:S(2)}) %all-to-all-start.2) | async-done | bytes 524320 | tf_op jit(solution)/shard_map/all_to_all | solution.py:76
  331.5 3.6 gather_fusion.3
  335.0 2.5 reshape.126
  337.5 3.7 fusion.53
  341.3 1.3 fusion.24
  342.7 16.3 %psum.31 = f32[128,6]{0,1:T(8,128)S(1)} all-reduce(f32[128,6]{0,1:T(8,128)S(1)} %bitcast_multiply_fusion), channel_id=1, replica_groups=mesh['sec'=64,'mp'=8] {'mp'}, use_global_device_ids=true, to_apply=%region_10.11 | all-reduce | flops 768 | bytes 6144 | tf_op jit(solution)/shard_map/psum | solution.py:89
  358.9 1.0 fusion.45
  360.0 6.1 %fusion.8 = bf16[128,2048]{1,0:T(8,128)(2,1)} fusion(f32[128,2048]{1,0:T(8,128)S(1)} %fusion.45, bf16[1,2048,1024]{2,1,0:T(8,128)(2,1)} %all-gather.3.cloned.1.call-done, f32[128,1024]{1,0:T(8,128)} %get-tuple-element.28, bf16[128,1,1024]{2,1,0:T(2,128)(2,1)} %get-tuple-element.16, bf16[128,1,1024]{2,1,0:T(2,128)(2,1)} %get-tuple-element.12, ...), kind=kOutput, calls=%fused_computation.11 | convolution fusion | flops 540803072 | bytes 7867392 | tf_op jit(solution)/shard_map/dot_general | solution.py:94
  366.1 36.4 %reduce-scatter.2.cloned.1.call-done = bf16[128,256]{1,0:T(8,128)(2,1)} async-done(((bf16[128,2048]{1,0:T(8,128)(2,1)}), bf16[128,256]{1,0:T(8,128)(2,1)}) %reduce-scatter.2.cloned.1.call-update) | async-done | bytes 65552 | tf_op jit(solution)/shard_map/reduce_scatter | solution.py:97
  (53 shorter events, 9.1 us)
Async XLA Ops:
  6.5 204.0 %copy-start = (bf16[1,1024,512]{2,1,0:T(8,128)(2,1)S(1)}, bf16[1,1024,512]{2,1,0:T(8,128)(2,1)}, u32[]{:S(2)}) copy-start(bf16[1,1024,512]{2,1,0:T(8,128)(2,1)} %param.11) | copy-start | bytes 3145732
  6.5 92.1 %copy-start.4 = (bf16[128,2048]{1,0:T(8,128)(2,1)S(1)}, bf16[128,2048]{1,0:T(8,128)(2,1)}, u32[]{:S(2)}) copy-start(bf16[128,2048]{1,0:T(8,128)(2,1)} %param.8) | copy-start | bytes 1572868
  6.5 11.1 %copy-start.1 = (s32[128,6]{0,1:T(8,128)S(1)}, s32[128,6]{0,1:T(8,128)}, u32[]{:S(2)}) copy-start(s32[128,6]{0,1:T(8,128)} %param.15) | copy-start | bytes 9220
  6.5 92.0 %all-gather.3.cloned.1.call-start = ((), (), s32[]{:S(2)}) async-start(), calls=%async_computation.7 | async-start | bytes 4259840 | tf_op jit(solution)/shard_map/all_gather | solution.py:28
  7.3 176.2 %all-reduce.4.cloned.1.call-start = ((), (), s32[]{:S(2)}) async-start(), calls=%async_computation.4 | async-start | bytes 1048576 | tf_op jit(solution)/shard_map/psum | solution.py:51
  103.5 90.3 %copy-start.3 = (bf16[1,512]{1,0:T(2,128)(2,1)S(1)}, bf16[1,512]{1,0:T(2,128)(2,1)}, u32[]{:S(2)}) copy-start(bf16[1,512]{1,0:T(2,128)(2,1)} %param.12) | copy-start | bytes 3076
  183.4 26.9 %all-to-all-start.1 = ((bf16[64,4,1024]{2,1,0:T(4,128)(2,1)}), bf16[64,4,1024]{2,1,0:T(4,128)(2,1)S(1)}, u32[]{:S(2)}, u32[]{:S(2)}) async-start(bf16[64,4,1024]{2,1,0:T(4,128)(2,1)} %all-reduce.4.cloned.1.call-done), calls=%async_computation.1 | async-start | bytes 1048576 | tf_op jit(solution)/shard_map/all_to_all | solution.py:53
  193.7 110.6 %all-reduce.6.cloned.1.call-start = ((), (), s32[]{:S(2)}) async-start(), calls=%async_computation.5 | async-start | bytes 1048576 | tf_op jit(solution)/shard_map/psum | solution.py:75
  228.1 87.0 %copy-start.2 = (bf16[2048,6,8]{0,2,1:T(8,128)(2,1)S(1)}, bf16[2048,6,8]{0,2,1:T(8,128)(2,1)}, u32[]{:S(2)}) copy-start(bf16[2048,6,8]{0,2,1:T(8,128)(2,1)} %param.10) | copy-start | bytes 589828
  304.4 26.9 %all-to-all-start.2 = ((bf16[64,4,1024]{2,1,0:T(4,128)(2,1)}), bf16[64,4,1024]{2,1,0:T(4,128)(2,1)S(1)}, u32[]{:S(2)}, u32[]{:S(2)}) async-start(bf16[64,4,1024]{2,1,0:T(4,128)(2,1)} %all-reduce.6.cloned.1.call-done), calls=%async_computation.2 | async-start | bytes 1048576 | tf_op jit(solution)/shard_map/all_to_all | solution.py:76
  314.6 87.9 %reduce-scatter.2.cloned.1.call-start = ((), (), s32[]{:S(2)}) async-start(), calls=%async_computation.6 | async-start | bytes 589824 | tf_op jit(solution)/shard_map/reduce_scatter | solution.py:97
Sparse Core Ops, SparseCore 0:
  10.7 87.8 all-gather.2
  104.9 78.5 all-reduce.3
  229.2 75.0 all-reduce.5
  366.2 36.2 reduce-scatter.1
where the time goes:
time: 410 us; the launch traced here: 409 us
  waiting for transfers between devices  286 us (70%)
  blocking collectives  48.5 us (12%)
  local copies, waits for them, and re-layouts  21.5 us (5%)
  starting transfers between devices  20.9 us (5%)
  matrix products  14.9 us (4%)
  between operations  13.4 us (3%)
    all_gather x1, waiting for transfers between devices, per_device(): whole_w = lax.all_gather(local_w, 'sec', axis=0, tiled=True)  79.5 us
    psum x1, waiting for transfers between devices, per_device(): grads = lax.psum(back.astype(jnp.bfloat16), 'mp')  75.2 us
    psum x1, waiting for transfers between devices, per_device(): sent = lax.psum(contrib.astype(jnp.bfloat16), 'mp')  62.6 us
    reduce_scatter x1, waiting for transfers between devices, per_device(): lax.psum_scatter((input_part + gate_part).astype(jnp.bfloat16), 'mp', sca...  36.4 us
    psum x1, blocking collectives, per_device(): logit = lax.psum(partial_logit, 'mp')  16.3 us
    psum x1, blocking collectives, per_device(): spread_sum = lax.psum(mine * gate_grad, 'mp')  16.3 us
    all_to_all x1, waiting for transfers between devices, per_device(): lax.all_to_all(sent.reshape(n_sec, pair_slots, -1), 'sec', split_axis=0,...  16.1 us
    all_to_all x1, blocking collectives, per_device(): lax.all_to_all(tag_out.reshape(n_sec, pair_slots), 'sec', split_axis=0, c...  16 us
  transfers between devices with their start and end apart: 6, of which 6 were waited for; matrix products, arithmetic and copies ran while one was open for 3% of the time, Pallas kernels for 0%

commit v1 on v0

--- a/solution.py
+++ b/solution.py
@@ -1,9 +1,17 @@
+import functools
 import jax
 import jax.numpy as jnp
 from jax import lax
 from jax.sharding import PartitionSpec as P
 
 loss_scale = 64.0
+
+
+def perform_modes(content, axis_name):
+    return jnp.sum(lax.all_gather(content, axis_name=axis_name), 0)
+
+
+bars_store = functools.partial(perform_modes, axis_name="mp")
 
 
 def silu_slope(value, sig):
@@ -72,7 +80,7 @@
     back = lax.dot_general(
         act_grad, up_local, (((1,), (1,)), ((), ())), preferred_element_type=jnp.float32
     )
-    grads = lax.psum(back.astype(jnp.bfloat16), "mp")
+    grads = bars_store(back.astype(jnp.bfloat16))
     returned = lax.all_to_all(
         grads.reshape(n_sec, pair_slots, -1), "sec", split_axis=0, concat_axis=0, tiled=True
     ).reshape(slots, -1)

time: 410 us -> 392 us (0.956)
  waiting for transfers between devices: 286 us -> 265 us
    psum x1 -> x0, waiting for transfers between devices: 75.2 us -> none  [per_device(): grads = lax.psum(back.astype(jnp.bfloat16), 'mp')]
    all_gather x0 -> x1, waiting for transfers between devices: none -> 53.4 us  [perform_modes(): return jnp.sum(lax.all_gather(content, axis_name=axis_name), 0)]
where the time goes in v1:
time: 392 us; the launch traced here: 391 us
  waiting for transfers between devices  265 us (68%)
  blocking collectives  47.7 us (12%)
  local copies, waits for them, and re-layouts  21.5 us (5%)
  starting transfers between devices  20.8 us (5%)
  matrix products  15.8 us (4%)
  between operations  13.4 us (3%)
  other arithmetic  6.75 us (2%)
    all_gather x1, waiting for transfers between devices, per_device(): whole_w = lax.all_gather(local_w, 'sec', axis=0, tiled=True)  79.5 us
    psum x1, waiting for transfers between devices, per_device(): sent = lax.psum(contrib.astype(jnp.bfloat16), 'mp')  62.6 us
    all_gather x1, waiting for transfers between devices, perform_modes(): return jnp.sum(lax.all_gather(content, axis_name=axis_name), 0)  53.4 us
    reduce_scatter x1, waiting for transfers between devices, per_device(): lax.psum_scatter((input_part + gate_part).astype(jnp.bfloat16), 'mp', sca...  37.3 us
    psum x1, blocking collectives, per_device(): logit = lax.psum(partial_logit, 'mp')  16.2 us
    all_to_all x1, waiting for transfers between devices, per_device(): lax.all_to_all(sent.reshape(n_sec, pair_slots, -1), 'sec', split_axis=0,...  16.1 us
    all_to_all x1, blocking collectives, per_device(): lax.all_to_all(tag_out.reshape(n_sec, pair_slots), 'sec', split_axis=0, c...  16 us
    all_to_all x1, waiting for transfers between devices, per_device(): lax.all_to_all(grads.reshape(n_sec, pair_slots, -1), 'sec', split_axis=0,...  15.5 us
  transfers between devices with their start and end apart: 6, of which 6 were waited for; matrix products, arithmetic and copies ran while one was open for 3% of the time, Pallas kernels for 0%

profile of v1, /device:TPU:2, one launch (start us, length us, event | category | flops | bytes accessed | tf_op | source)
XLA Modules:
  0.0 391.1 jit_solution(6233275253377874821)
XLA Ops:
  9.9 1.3 compare_select_fusion
  11.4 3.4 scatter_custom_fusion
  14.8 1.4 fusion.54
  16.3 1.4 gather_fusion.1
  17.6 1.4 gather_fusion
  19.1 79.5 %all-gather.5.cloned.1.call-done = bf16[1,2048,1024]{2,1,0:T(8,128)(2,1)} async-done(((bf16[1,32,1024]{2,1,0:T(8,128)(2,1)}), bf16[1,2048,1024]{2,1,0:T(8,128)(2,1)}) %all-gather.5.cloned.1.call-update) | async-done | bytes 4194320 | tf_op jit(solution)/shard_map/all_gather | solution.py:36
  98.6 3.8 multiply_convert_fusion.2
  104.9 16.0 %all_to_all.20 = bf16[64,1,4]{2,1,0:T(2,128)(2,1)S(1)} all-to-all(bf16[64,1,4]{2,1,0:T(2,128)(2,1)S(1)} %all_to_all.16), channel_id=1, replica_groups=mesh['sec'=64,'mp'=8] {'sec'}, dimensions={0} | all-to-all | bytes 1024 | tf_op jit(solution)/shard_map/all_to_all | solution.py:64
  120.9 62.6 %all-reduce.3.cloned.1.call-done = bf16[64,4,1024]{2,1,0:T(4,128)(2,1)} async-done(((bf16[64,4,1024]{2,1,0:T(4,128)(2,1)}), bf16[64,4,1024]{2,1,0:T(4,128)(2,1)}) %all-reduce.3.cloned.1.call-update) | async-done | bytes 524304 | tf_op jit(solution)/shard_map/psum | solution.py:59
  183.5 10.3 %all-to-all-start.1 = ((bf16[64,4,1024]{2,1,0:T(4,128)(2,1)}), bf16[64,4,1024]{2,1,0:T(4,128)(2,1)S(1)}, u32[]{:S(2)}, u32[]{:S(2)}) async-start(bf16[64,4,1024]{2,1,0:T(4,128)(2,1)} %all-reduce.3.cloned.1.call-done), calls=%async_computation.1 | async-start | bytes 1048576 | tf_op jit(solution)/shard_map/all_to_all | solution.py:61
  194.3 16.1 %all-to-all-done.1 = bf16[64,4,1024]{2,1,0:T(4,128)(2,1)S(1)} async-done(((bf16[64,4,1024]{2,1,0:T(4,128)(2,1)}), bf16[64,4,1024]{2,1,0:T(4,128)(2,1)S(1)}, u32[]{:S(2)}, u32[]{:S(2)}) %all-to-all-start.1) | async-done | bytes 524320 | tf_op jit(solution)/shard_map/all_to_all | solution.py:61
  211.2 16.2 %psum.22 = f32[256]{0:T(256)S(1)} all-reduce(f32[256]{0:T(256)S(1)} %get-tuple-element.29), channel_id=1, replica_groups=mesh['sec'=64,'mp'=8] {'mp'}, use_global_device_ids=true, to_apply=%region_8.9 | all-reduce | flops 256 | bytes 2048 | tf_op jit(solution)/shard_map/psum | solution.py:74
  227.4 1.5 convolution_convert_fusion
  228.9 53.4 %all-gather.7.cloned.1.call-done = bf16[2048,1024]{1,0:T(8,128)(2,1)} async-done(((bf16[256,1024]{1,0:T(8,128)(2,1)}), bf16[2048,1024]{1,0:T(8,128)(2,1)}) %all-gather.7.cloned.1.call-update) | async-done | bytes 4194320 | tf_op jit(solution)/shard_map/all_gather | solution.py:11
  282.3 3.1 reduce_sum.71
  286.4 10.3 %all-to-all-start.2 = ((bf16[64,4,1024]{2,1,0:T(4,128)(2,1)}), bf16[64,4,1024]{2,1,0:T(4,128)(2,1)S(1)}, u32[]{:S(2)}, u32[]{:S(2)}) async-start(bf16[64,4,1024]{2,1,0:T(4,128)(2,1)} %reshape.96), calls=%async_computation.2 | async-start | bytes 1048576 | tf_op jit(solution)/shard_map/all_to_all | solution.py:84
  297.9 15.5 %all-to-all-done.2 = bf16[64,4,1024]{2,1,0:T(4,128)(2,1)S(1)} async-done(((bf16[64,4,1024]{2,1,0:T(4,128)(2,1)}), bf16[64,4,1024]{2,1,0:T(4,128)(2,1)S(1)}, u32[]{:S(2)}, u32[]{:S(2)}) %all-to-all-start.2) | async-done | bytes 524320 | tf_op jit(solution)/shard_map/all_to_all | solution.py:84
  313.5 3.6 gather_fusion.3
  317.1 2.5 reshape.126
  319.6 3.7 fusion.53
  323.3 1.3 fusion.24
  324.7 15.4 %psum.23 = f32[128,6]{0,1:T(8,128)S(1)} all-reduce(f32[128,6]{0,1:T(8,128)S(1)} %bitcast_multiply_fusion), channel_id=1, replica_groups=mesh['sec'=64,'mp'=8] {'mp'}, use_global_device_ids=true, to_apply=%region_10.11 | all-reduce | flops 768 | bytes 6144 | tf_op jit(solution)/shard_map/psum | solution.py:97
  341.2 6.1 %fusion.8 = bf16[128,2048]{1,0:T(8,128)(2,1)} fusion(f32[128,2048]{1,0:T(8,128)S(1)} %fusion.45, bf16[1,2048,1024]{2,1,0:T(8,128)(2,1)} %all-gather.5.cloned.1.call-done, f32[128,1024]{1,0:T(8,128)} %get-tuple-element.28, bf16[128,1,1024]{2,1,0:T(2,128)(2,1)} %get-tuple-element.16, bf16[128,1,1024]{2,1,0:T(2,128)(2,1)} %get-tuple-element.12, ...), kind=kOutput, calls=%fused_computation.11 | convolution fusion | flops 540803072 | bytes 7867392 | tf_op jit(solution)/shard_map/dot_general | solution.py:102
  347.3 37.3 %reduce-scatter.2.cloned.1.call-done = bf16[128,256]{1,0:T(8,128)(2,1)} async-done(((bf16[128,2048]{1,0:T(8,128)(2,1)}), bf16[128,256]{1,0:T(8,128)(2,1)}) %reduce-scatter.2.cloned.1.call-update) | async-done | bytes 65552 | tf_op jit(solution)/shard_map/reduce_scatter | solution.py:105
  (54 shorter events, 10.7 us)
Async XLA Ops:
  6.5 204.0 %copy-start = (bf16[1,1024,512]{2,1,0:T(8,128)(2,1)S(1)}, bf16[1,1024,512]{2,1,0:T(8,128)(2,1)}, u32[]{:S(2)}) copy-start(bf16[1,1024,512]{2,1,0:T(8,128)(2,1)} %param.11) | copy-start | bytes 3145732
  6.5 92.1 %copy-start.4 = (bf16[128,2048]{1,0:T(8,128)(2,1)S(1)}, bf16[128,2048]{1,0:T(8,128)(2,1)}, u32[]{:S(2)}) copy-start(bf16[128,2048]{1,0:T(8,128)(2,1)} %param.8) | copy-start | bytes 1572868
  6.5 11.1 %copy-start.1 = (s32[128,6]{0,1:T(8,128)S(1)}, s32[128,6]{0,1:T(8,128)}, u32[]{:S(2)}) copy-start(s32[128,6]{0,1:T(8,128)} %param.15) | copy-start | bytes 9220
  6.5 92.0 %all-gather.5.cloned.1.call-start = ((), (), s32[]{:S(2)}) async-start(), calls=%async_computation.6 | async-start | bytes 4259840 | tf_op jit(solution)/shard_map/all_gather | solution.py:36
  7.3 176.2 %all-reduce.3.cloned.1.call-start = ((), (), s32[]{:S(2)}) async-start(), calls=%async_computation.4 | async-start | bytes 1048576 | tf_op jit(solution)/shard_map/psum | solution.py:59
  103.6 90.3 %copy-start.3 = (bf16[1,512]{1,0:T(2,128)(2,1)S(1)}, bf16[1,512]{1,0:T(2,128)(2,1)}, u32[]{:S(2)}) copy-start(bf16[1,512]{1,0:T(2,128)(2,1)} %param.12) | copy-start | bytes 3076
  183.5 26.9 %all-to-all-start.1 = ((bf16[64,4,1024]{2,1,0:T(4,128)(2,1)}), bf16[64,4,1024]{2,1,0:T(4,128)(2,1)S(1)}, u32[]{:S(2)}, u32[]{:S(2)}) async-start(bf16[64,4,1024]{2,1,0:T(4,128)(2,1)} %all-reduce.3.cloned.1.call-done), calls=%async_computation.1 | async-start | bytes 1048576 | tf_op jit(solution)/shard_map/all_to_all | solution.py:61
  193.8 88.6 %all-gather.7.cloned.1.call-start = ((), (), s32[]{:S(2)}) async-start(), calls=%async_computation.7 | async-start | bytes 4718592 | tf_op jit(solution)/shard_map/all_gather | solution.py:11
  285.4 11.7 %copy-start.2 = (bf16[2048,6,8]{0,2,1:T(8,128)(2,1)S(1)}, bf16[2048,6,8]{0,2,1:T(8,128)(2,1)}, u32[]{:S(2)}) copy-start(bf16[2048,6,8]{0,2,1:T(8,128)(2,1)} %param.10) | copy-start | bytes 589828
  286.4 26.9 %all-to-all-start.2 = ((bf16[64,4,1024]{2,1,0:T(4,128)(2,1)}), bf16[64,4,1024]{2,1,0:T(4,128)(2,1)S(1)}, u32[]{:S(2)}, u32[]{:S(2)}) async-start(bf16[64,4,1024]{2,1,0:T(4,128)(2,1)} %reshape.96), calls=%async_computation.2 | async-start | bytes 1048576 | tf_op jit(solution)/shard_map/all_to_all | solution.py:84
  296.7 87.9 %reduce-scatter.2.cloned.1.call-start = ((), (), s32[]{:S(2)}) async-start(), calls=%async_computation.5 | async-start | bytes 589824 | tf_op jit(solution)/shard_map/reduce_scatter | solution.py:105
Sparse Core Ops, SparseCore 0:
  10.7 87.8 all-gather.4
  104.9 78.5 all-reduce.2
  229.0 53.2 all-gather.6
  347.4 37.0 reduce-scatter.1
